TPU v7x, 128 devices: a whole 4x4x4 slice. The times are simulated.
128 devices in a mesh: row: 8 (over z, core), col: 16 (over y, x).
Axes of the slice: x: 4, y: 4, z: 4, core: 2. Of those that a mesh axis runs over, the one named last changes fastest.
Arguments:
- tokens: bfloat16 [512, 8192], P('row', 'col'), may hold values from -6 to 6
- weights: bfloat16 [2, 8192, 28672], P(None, 'col', 'row'), may hold values from -2 to 2
- adapter_in: bfloat16 [2, 64, 8192], P(None, None, 'col'), may hold values from -0.75 to 0.75
- adapter_out: bfloat16 [2, 64, 28672], P(None, None, 'row'), may hold values from -0.3 to 0.3
- magnitude: float32 [2, 28672], P(None, 'row'), may hold values from 0.5 to 2
- hidden_cot: bfloat16 [512, 28672], P('col', 'row'), may hold values from -0.29882812 to 0.29882812
Outputs:
- hidden: bfloat16 [512, 28672], P('col', 'row')
- grad_in: float32 [2, 64, 8192], P(None, None, 'col')
- grad_out: float32 [2, 64, 28672], P(None, None, 'row')
- grad_mag: float32 [2, 28672], P(None, 'row')
All inputs are finite; a program needn't handle non-finite values.
Results may differ from a plain program's by a relative error of at most 0.028.
Values may be sent and summed in bfloat16 or wider, within the bound.
A program may use at most 192 MiB of HBM per device.

v0:
```python
import jax
import jax.numpy as jnp
from jax import lax
from jax.sharding import PartitionSpec as P

EPSILON = 1e-06


def copy_for_each(value, axis):
    copies = jnp.broadcast_to(value, (lax.axis_size(axis), *value.shape))
    return lax.all_to_all(copies, axis, split_axis=0, concat_axis=0, tiled=True)


def over_copies(value, axis):
    everything = copy_for_each(value, axis)
    return jnp.sum(everything, axis=0)


def laid_out(pieces, dim):
    lengths = list(pieces.shape[1:])
    lengths[dim] *= pieces.shape[0]
    return jnp.moveaxis(pieces, 0, dim).reshape(lengths)


def gathered_copies(value, axis, dim):
    return laid_out(copy_for_each(value, axis), dim)


def of_everyone(value, axis):
    return copy_for_each(value, axis).astype(jnp.float32).sum(axis=0)


def cotangents(gate, up_proj, cot_rows):
    sigmoid_g = jax.nn.sigmoid(gate)
    cot_float = cot_rows.astype(jnp.float32)
    d_gate = (cot_float * up_proj * sigmoid_g * (1.0 + gate * (1.0 - sigmoid_g))).astype(
        jnp.bfloat16
    )
    d_up = (cot_float * gate * sigmoid_g).astype(jnp.bfloat16)
    return (d_gate, d_up)


def on_device(tokens, weights, adapter_in, adapter_out, magnitude, hidden_cot):
    in_float = adapter_in.astype(jnp.float32)
    out_float = adapter_out.astype(jnp.float32)
    low_rank = jnp.einsum(
        "prd,prf->pdf", adapter_in, adapter_out, preferred_element_type=jnp.float32
    )
    direction = weights.astype(jnp.float32) + low_rank
    square_sum = over_copies(jnp.sum(direction * direction, axis=1), "col")
    column_norm = jnp.sqrt(square_sum + EPSILON)
    merged = (direction * (magnitude / column_norm)[:, None, :]).astype(jnp.bfloat16)
    token_all = gathered_copies(tokens, "row", 0)
    share_rows = token_all.shape[0] // lax.axis_size("col")
    partial_value = jnp.einsum("td,pdf->ptf", token_all, merged, preferred_element_type=jnp.float32)
    summed = lax.psum(partial_value.astype(jnp.bfloat16), "col").astype(jnp.float32)
    gate, up_proj = (summed[0], summed[1])
    hidden_all = (gate * jax.nn.sigmoid(gate) * up_proj).astype(jnp.bfloat16)
    hidden = lax.dynamic_slice_in_dim(hidden_all, lax.axis_index("col") * share_rows, share_rows, 0)
    cot_all = lax.all_gather(hidden_cot, "col", axis=0, tiled=True)
    d_gate, d_up = cotangents(gate, up_proj, cot_all)
    d_stack = jnp.stack((d_gate, d_up), axis=0)
    grad_weight = jnp.einsum("td,ptf->pdf", token_all, d_stack, preferred_element_type=jnp.float32)
    coef_grad = magnitude / column_norm
    statistic = over_copies(jnp.sum(grad_weight * direction, axis=1), "col")
    coef_dir = magnitude * statistic / column_norm**3
    d_direction = coef_grad[:, None, :] * grad_weight - coef_dir[:, None, :] * direction
    right_part = jnp.einsum("prd,pdf->prf", in_float, d_direction, precision=lax.Precision.HIGHEST)
    grad_out = lax.psum(right_part.astype(jnp.bfloat16), "col").astype(jnp.float32)
    left_part = jnp.einsum("prf,pdf->prd", out_float, d_direction, precision=lax.Precision.HIGHEST)
    grad_in = of_everyone(left_part.astype(jnp.bfloat16), "row").astype(jnp.float32)
    grad_mag = statistic / column_norm
    return (hidden, grad_in, grad_out, grad_mag)


def solution(mesh):
    in_specs = (
        P("row", "col"),
        P(None, "col", "row"),
        P(None, None, "col"),
        P(None, None, "row"),
        P(None, "row"),
        P("col", "row"),
    )
    out_specs = (P("col", "row"), P(None, None, "col"), P(None, None, "row"), P(None, "row"))
    return jax.shard_map(
        on_device, mesh=mesh, in_specs=in_specs, out_specs=out_specs, check_vma=False
    )
```

profile of v0, /device:TPU:0, one launch (start us, length us, event | category | flops | bytes accessed | tf_op | source)
XLA Modules:
  0.0 371.1 jit_solution(17381849521522753354)
XLA Ops:
  7.2 0.7 all-gather.2.cloned.1.call-update
  7.9 0.4 copy-done
  8.4 8.6 %multiply_reduce_fusion = (f32[2,3584]{1,0:T(2,128)S(1)}, f32[2,512,3584]{2,1,0:T(8,128)}) fusion(bf16[2,64,512]{2,1,0:T(8,128)(2,1)} %param.8, bf16[2,64,3584]{2,1,0:T(8,128)(2,1)S(1)} %copy-done, bf16[2,512,3584]{2,1,0:T(8,128)(2,1)} %param.7), kind=kOutput, calls=%fused_computation.5 | convolution fusion | flops 484434944 | bytes 23097344 | tf_op jit(solution)/shard_map/prd,prf->pdf/dot_general | solution.py:46
  17.0 0.1 broadcast_in_dim.15
  17.1 19.8 %all_to_all.20 = f32[16,2,3584]{2,1,0:T(2,128)S(1)} all-to-all(f32[16,2,3584]{2,1,0:T(2,128)S(1)} %broadcast_in_dim.15), channel_id=1, replica_groups=mesh['row'=8,'col'=16] {'col'}, dimensions={0} | all-to-all | bytes 917504 | tf_op jit(solution)/shard_map/all_to_all | solution.py:11
  36.9 0.8 broadcast_in_dim.16
  37.8 5.2 %all-to-all-start.1 = ((bf16[8,64,512]{2,1,0:T(8,128)(2,1)}), bf16[8,64,512]{2,1,0:T(8,128)(2,1)S(1)}, u32[]{:S(2)}, u32[]{:S(2)}) async-start(bf16[8,64,512]{2,1,0:T(8,128)(2,1)} %broadcast_in_dim.16), calls=%async_computation.1 | async-start | bytes 1048576 | tf_op jit(solution)/shard_map/all_to_all | solution.py:11
  43.0 0.1 reduce_sum.46
  43.3 10.1 %all-to-all-done.1 = bf16[8,64,512]{2,1,0:T(8,128)(2,1)S(1)} async-done(((bf16[8,64,512]{2,1,0:T(8,128)(2,1)}), bf16[8,64,512]{2,1,0:T(8,128)(2,1)S(1)}, u32[]{:S(2)}, u32[]{:S(2)}) %all-to-all-start.1) | async-done | bytes 524320 | tf_op jit(solution)/shard_map/all_to_all | solution.py:11
  53.3 11.6 %fusion.12 = bf16[2,512,3584]{1,2,0:T(8,128)(2,1)} fusion(bf16[512,512,1]{1,0,2:T(8,128)(2,1)S(1)} %bitcast.53, f32[2,512,3584]{2,1,0:T(8,128)} %get-tuple-element.28, f32[2,3584]{1,0:T(2,128)S(1)} %fusion.30), kind=kOutput, calls=%fused_computation.23 | convolution fusion | flops 3769106432 | bytes 22573056 | tf_op jit(solution)/shard_map/td,pdf->ptf/dot_general | solution.py:55
  64.9 0.7 all-gather.2.cloned.1.call-done
  65.6 5.9 %copy.27 = bf16[512,3584]{0,1:T(8,128)(2,1)} copy(bf16[512,3584]{1,0:T(8,128)(2,1)} %all-gather.2.cloned.1.call-done) | data formatting | bytes 7340032 | tf_op jit(solution)/shard_map/all_gather | solution.py:60
  71.5 128.1 %all-reduce.3.cloned.1.call-done = bf16[2,512,3584]{1,2,0:T(8,128)(2,1)} async-done(((bf16[2,512,3584]{1,2,0:T(8,128)(2,1)}), bf16[2,512,3584]{1,2,0:T(8,128)(2,1)}) %all-reduce.3.cloned.1.call-update) | async-done | bytes 7340048 | tf_op jit(solution)/shard_map/psum | solution.py:56
  199.7 10.3 %convert_element_type.51 = f32[2,512,3584]{1,2,0:T(8,128)} convert(bf16[2,512,3584]{1,2,0:T(8,128)(2,1)} %all-reduce.3.cloned.1.call-done) | non-fusion elementwise | flops 3670016 | bytes 22020096 | tf_op jit(solution)/shard_map/convert_element_type | solution.py:56
  210.0 9.8 %fusion.20 = (bf16[1,512,3584]{1,2,0:T(8,128)(2,1)S(1)}, bf16[1,512,3584]{1,2,0:T(8,128)(2,1)S(1)}, f32[512,3584]{0,1:T(8,128)}) fusion(bf16[512,3584]{0,1:T(8,128)(2,1)} %copy.27, f32[2,512,3584]{1,2,0:T(8,128)} %convert_element_type.51), kind=kLoop, calls=%fused_computation.28 | loop fusion | flops 25690112 | bytes 33030144 | tf_op jit(solution)/shard_map/stack | solution.py:62
  219.8 10.6 %fusion.1 = (f32[2,3584]{1,0:T(2,128)S(1)}, f32[2,3584,512]{1,2,0:T(8,128)}) fusion(f32[2,512,3584]{2,1,0:T(8,128)} %get-tuple-element.28, bf16[512,512,1]{1,0,2:T(8,128)(2,1)S(1)} %bitcast.54, bf16[1,512,3584]{1,2,0:T(8,128)(2,1)S(1)} %get-tuple-element.21, bf16[1,512,3584]{1,2,0:T(8,128)(2,1)S(1)} %get-tuple-element.20), kind=kOutput, calls=%fused_computation.3 | convolution fusion | flops 3769099264 | bytes 37253120 | tf_op jit(solution)/shard_map/td,ptf->pdf/dot_general | solution.py:63
  230.4 0.9 broadcast_in_dim.17
  231.3 5.4 %all-to-all-start.2 = ((f32[16,2,3584]{2,1,0:T(2,128)}), f32[16,2,3584]{2,1,0:T(2,128)S(1)}, u32[]{:S(2)}, u32[]{:S(2)}) async-start(f32[16,2,3584]{2,1,0:T(2,128)} %broadcast_in_dim.17), calls=%async_computation.2 | async-start | bytes 917504 | tf_op jit(solution)/shard_map/all_to_all | solution.py:11
  236.7 0.2 all-reduce.5.cloned.1.call-start
  236.9 10.4 %all-to-all-done.2 = f32[16,2,3584]{2,1,0:T(2,128)S(1)} async-done(((f32[16,2,3584]{2,1,0:T(2,128)}), f32[16,2,3584]{2,1,0:T(2,128)S(1)}, u32[]{:S(2)}, u32[]{:S(2)}) %all-to-all-start.2) | async-done | bytes 458784 | tf_op jit(solution)/shard_map/all_to_all | solution.py:11
  247.3 0.7 reduce_sum.48
  248.1 1.4 fusion.29
  249.5 14.3 %fusion.25 = bf16[2,64,512]{2,1,0:T(8,128)(2,1)S(1)} fusion(bf16[2,64,3584]{2,1,0:T(8,128)(2,1)S(1)} %copy-done, f32[2,3584,512]{1,2,0:T(8,128)} %get-tuple-element.30, f32[2,512,3584]{2,1,0:T(8,128)} %get-tuple-element.28, f32[2,3584]{1,0:T(2,128)S(1)} %get-tuple-element.26, f32[2,3584]{1,0:T(2,128)S(1)} %fusion.30), kind=kOutput, calls=%fused_computation.34 | convolution fusion | flops 2829647872 | bytes 30466048 | tf_op jit(solution)/shard_map/prf,pdf->prd/dot_general | solution.py:70
  263.9 13.3 %fusion.16 = bf16[2,64,3584]{2,1,0:T(8,128)(2,1)} fusion(bf16[2,64,512]{2,1,0:T(8,128)(2,1)S(1)} %copy-done.1, f32[2,3584,512]{1,2,0:T(8,128)} %get-tuple-element.30, f32[2,512,3584]{2,1,0:T(8,128)S(1)} %bitcast.52, f32[2,3584]{1,0:T(2,128)S(1)} %get-tuple-element.26, f32[2,3584]{1,0:T(2,128)S(1)} %fusion.30), kind=kOutput, calls=%fused_computation.26 | convolution fusion | flops 2830041088 | bytes 30466048 | tf_op jit(solution)/shard_map/prd,pdf->prf/dot_general | solution.py:68
  277.2 1.2 broadcast_in_dim.18
  278.4 4.4 %all-to-all-start.3 = ((bf16[8,2,64,512]{3,2,1,0:T(8,128)(2,1)}), bf16[8,2,64,512]{3,2,1,0:T(8,128)(2,1)S(1)}, u32[]{:S(2)}, u32[]{:S(2)}) async-start(bf16[8,2,64,512]{3,2,1,0:T(8,128)(2,1)} %broadcast_in_dim.18), calls=%async_computation.3 | async-start | bytes 2097152 | tf_op jit(solution)/shard_map/all_to_all | solution.py:11
  282.8 12.3 %slice_bitcast_fusion.1 = (f32[512,3584]{0,1:T(8,128)}, f32[512,3584]{0,1:T(8,128)}) fusion(f32[2,512,3584]{1,2,0:T(8,128)} %convert_element_type.51), kind=kLoop, calls=%fused_computation.16 | loop fusion | bytes 29360128 | tf_op jit(solution)/shard_map/squeeze | solution.py:57
  295.1 4.2 %fusion.21 = bf16[32,3584]{0,1:T(8,128)(2,1)S(1)} fusion(f32[512,3584]{0,1:T(8,128)} %get-tuple-element.24, s32[]{:T(128)S(6)} %select_n.3, f32[512,3584]{0,1:T(8,128)} %get-tuple-element.22, f32[512,3584]{0,1:T(8,128)} %get-tuple-element.23), kind=kLoop, calls=%fused_computation.31 | loop fusion | flops 344064 | bytes 1605636 | tf_op jit(solution)/shard_map/convert_element_type | solution.py:58
  299.2 1.0 copy.31
  300.2 60.9 %all-reduce.5.cloned.1.call-done = bf16[2,64,3584]{2,1,0:T(8,128)(2,1)} async-done(((bf16[2,64,3584]{2,1,0:T(8,128)(2,1)}), bf16[2,64,3584]{2,1,0:T(8,128)(2,1)}) %all-reduce.5.cloned.1.call-update) | async-done | bytes 917520 | tf_op jit(solution)/shard_map/psum | solution.py:69
  361.1 2.6 convert_element_type.61
  363.7 0.8 convert_reduce_fusion
  (22 shorter events, 0.2 us)
Async XLA Ops:
  7.2 1.2 copy-start
  7.2 58.4 %all-gather.2.cloned.1.call-start = ((), (), s32[]{:S(2)}) async-start(), calls=%async_computation.5 | async-start | bytes 3899392 | tf_op jit(solution)/shard_map/all_gather | solution.py:60
  8.4 28.6 %copy-start.3 = (bf16[64,512]{1,0:T(8,128)(2,1)S(1)}, bf16[64,512]{1,0:T(8,128)(2,1)}, u32[]{:S(2)}) copy-start(bf16[64,512]{1,0:T(8,128)(2,1)} %param.6) | copy-start | bytes 196612
  8.4 34.8 %copy-start.2 = (f32[2,3584]{1,0:T(2,128)S(1)}, f32[2,3584]{1,0:T(2,128)}, u32[]{:S(2)}) copy-start(f32[2,3584]{1,0:T(2,128)} %param.10) | copy-start | bytes 86020
  37.8 15.5 %all-to-all-start.1 = ((bf16[8,64,512]{2,1,0:T(8,128)(2,1)}), bf16[8,64,512]{2,1,0:T(8,128)(2,1)S(1)}, u32[]{:S(2)}, u32[]{:S(2)}) async-start(bf16[8,64,512]{2,1,0:T(8,128)(2,1)} %broadcast_in_dim.16), calls=%async_computation.1 | async-start | bytes 1048576 | tf_op jit(solution)/shard_map/all_to_all | solution.py:11
  43.0 156.7 %all-reduce.3.cloned.1.call-start = ((), (), s32[]{:S(2)}) async-start(), calls=%async_computation.4 | async-start | bytes 14680064 | tf_op jit(solution)/shard_map/psum | solution.py:56
  230.4 33.4 %slice-start = ((s8[14680064]{0:T(1024)(128)(4,1)}), s8[2097152]{0:T(1024)(128)(4,1)S(1)}, s32[]{:S(2)}) async-start(s8[14680064]{0:T(1024)(128)(4,1)} %bitcast.51), calls=%async_computation.7 | async-start | bytes 4194304
  231.3 16.0 %all-to-all-start.2 = ((f32[16,2,3584]{2,1,0:T(2,128)}), f32[16,2,3584]{2,1,0:T(2,128)S(1)}, u32[]{:S(2)}, u32[]{:S(2)}) async-start(f32[16,2,3584]{2,1,0:T(2,128)} %broadcast_in_dim.17), calls=%async_computation.2 | async-start | bytes 917504 | tf_op jit(solution)/shard_map/all_to_all | solution.py:11
  236.7 124.4 %all-reduce.5.cloned.1.call-start = ((), (), s32[]{:S(2)}) async-start(), calls=%async_computation.6 | async-start | bytes 1835008 | tf_op jit(solution)/shard_map/psum | solution.py:69
  249.5 14.4 %slice-start.1 = ((s8[14680064]{0:T(1024)(128)(4,1)}), s8[4194304]{0:T(1024)(128)(4,1)S(1)}, s32[]{:S(2)}) async-start(s8[14680064]{0:T(1024)(128)(4,1)} %bitcast.51), calls=%async_computation.8 | async-start | bytes 8388608
  249.5 14.4 %slice-start.2 = ((s8[14680064]{0:T(1024)(128)(4,1)}), s8[4194304]{0:T(1024)(128)(4,1)S(1)}, s32[]{:S(2)}) async-start(s8[14680064]{0:T(1024)(128)(4,1)} %bitcast.51), calls=%async_computation.9 | async-start | bytes 8388608
  249.5 14.4 %slice-start.3 = ((s8[14680064]{0:T(1024)(128)(4,1)}), s8[4194304]{0:T(1024)(128)(4,1)S(1)}, s32[]{:S(2)}) async-start(s8[14680064]{0:T(1024)(128)(4,1)} %bitcast.51), calls=%async_computation.10 | async-start | bytes 8388608
  249.5 14.4 %copy-start.1 = (bf16[2,64,512]{2,1,0:T(8,128)(2,1)S(1)}, bf16[2,64,512]{2,1,0:T(8,128)(2,1)}, u32[]{:S(2)}) copy-start(bf16[2,64,512]{2,1,0:T(8,128)(2,1)} %param.8) | copy-start | bytes 393220
  278.4 85.3 %all-to-all-start.3 = ((bf16[8,2,64,512]{3,2,1,0:T(8,128)(2,1)}), bf16[8,2,64,512]{3,2,1,0:T(8,128)(2,1)S(1)}, u32[]{:S(2)}, u32[]{:S(2)}) async-start(bf16[8,2,64,512]{3,2,1,0:T(8,128)(2,1)} %broadcast_in_dim.18), calls=%async_computation.3 | async-start | bytes 2097152 | tf_op jit(solution)/shard_map/all_to_all | solution.py:11
Sparse Core Ops, SparseCore 0:
  10.1 55.4 all-gather.1
  69.1 130.5 all-reduce.2
  277.4 83.7 all-reduce.4
where the time goes:
time: 372 us; the launch traced here: 371 us
  waiting for transfers between devices  211 us (57%)
  matrix products  58.4 us (16%)
  other arithmetic  30.1 us (8%)
  local copies, waits for them, and re-layouts  22.6 us (6%)
  blocking collectives  19.8 us (5%)
  starting transfers between devices  15.3 us (4%)
  between operations  13.9 us (4%)
    psum x1, waiting for transfers between devices, on_device(): lax.psum(partial_value.astype(jnp.bfloat16), 'col').astype(jnp.float32)  128 us
    psum x1, waiting for transfers between devices, on_device(): lax.psum(right_part.astype(jnp.bfloat16), 'col').astype(jnp.float32)  60.9 us
    all_to_all x3, waiting for transfers between devices, copy_for_each(): return lax.all_to_all(copies, axis, split_axis=0, concat_axis=0, tiled=True)  20.5 us
    all_to_all x1, blocking collectives, copy_for_each(): return lax.all_to_all(copies, axis, split_axis=0, concat_axis=0, tiled=True)  19.8 us
    all_to_all x3, starting transfers between devices, copy_for_each(): return lax.all_to_all(copies, axis, split_axis=0, concat_axis=0, tiled=True)  15 us
    dot_general x1, matrix products, on_device(): jnp.einsum('prf,pdf->prd', out_float, d_direction, precision=lax.Precisio...  14.3 us
    dot_general x1, matrix products, on_device(): jnp.einsum('prd,pdf->prf', in_float, d_direction, precision=lax.Precision...  13.3 us
    squeeze x1, local copies, waits for them, and re-layouts, on_device(): gate, up_proj = (summed[0], summed[1])  12.3 us
  transfers between devices with their start and end apart: 6, of which 5 were waited for; matrix products, arithmetic and copies ran while one was open for 13% of the time, Pallas kernels for 0%

commit v1 on v0

--- a/solution.py
+++ b/solution.py
@@ -53,7 +53,9 @@
     token_all = gathered_copies(tokens, "row", 0)
     share_rows = token_all.shape[0] // lax.axis_size("col")
     partial_value = jnp.einsum("td,pdf->ptf", token_all, merged, preferred_element_type=jnp.float32)
-    summed = lax.psum(partial_value.astype(jnp.bfloat16), "col").astype(jnp.float32)
+    summed = jnp.sum(lax.all_gather(partial_value.astype(jnp.bfloat16), "col"), axis=0).astype(
+        jnp.float32
+    )
     gate, up_proj = (summed[0], summed[1])
     hidden_all = (gate * jax.nn.sigmoid(gate) * up_proj).astype(jnp.bfloat16)
     hidden = lax.dynamic_slice_in_dim(hidden_all, lax.axis_index("col") * share_rows, share_rows, 0)

time: 372 us -> 906 us (2.44)
  waiting for transfers between devices: 211 us -> 705 us
  other arithmetic: 30.1 us -> 68 us
    all_gather x0 -> x1, waiting for transfers between devices: none -> 620 us  [on_device(): lax.all_gather(partial_value.astype(jnp.bfloat16), 'col')]
    psum x1 -> x0, waiting for transfers between devices: 128 us -> none  [on_device(): lax.psum(partial_value.astype(jnp.bfloat16), 'col').astype(jnp.float32)]
    reduce_sum x0 -> x1, other arithmetic: none -> 41.3 us  [on_device(): jnp.sum(lax.all_gather(partial_value.astype(jnp.bfloat16), 'col'), axis=0)]
    convert_element_type x0 -> x1, local copies, waits for them, and re-layouts: none -> 9.98 us  [on_device(): partial_value.astype(jnp.bfloat16)]
  transfers between devices with their start and end apart: 6 -> 6, of which waited for: 5 -> 4; matrix products, arithmetic and copies ran while one was open for 13% -> 8% of each run, Pallas kernels for 0% -> 0%
where the time goes in v1:
time: 906 us; the launch traced here: 905 us
  waiting for transfers between devices  705 us (78%)
  other arithmetic  68 us (8%)
  matrix products  58.8 us (6%)
  local copies, waits for them, and re-layouts  25.6 us (3%)
  blocking collectives  17.7 us (2%)
  starting transfers between devices  15.5 us (2%)
  between operations  13.8 us (2%)
    all_gather x1, waiting for transfers between devices, on_device(): lax.all_gather(partial_value.astype(jnp.bfloat16), 'col')  620 us
    psum x1, waiting for transfers between devices, on_device(): lax.psum(right_part.astype(jnp.bfloat16), 'col').astype(jnp.float32)  64.8 us
    reduce_sum x1, other arithmetic, on_device(): jnp.sum(lax.all_gather(partial_value.astype(jnp.bfloat16), 'col'), axis=0)  41.3 us
    all_to_all x3, waiting for transfers between devices, copy_for_each(): return lax.all_to_all(copies, axis, split_axis=0, concat_axis=0, tiled=True)  20.4 us
  transfers between devices with their start and end apart: 6, of which 4 were waited for; matrix products, arithmetic and copies ran while one was open for 8% of the time, Pallas kernels for 0%

profile of v1, /device:TPU:0, one launch (start us, length us, event | category | flops | bytes accessed | tf_op | source)
XLA Modules:
  0.0 904.9 jit_solution(647256329067684743)
XLA Ops:
  7.2 1.2 copy-done
  8.4 8.6 multiply_reduce_fusion
  17.0 0.1 broadcast_in_dim.15
  17.1 17.7 %all_to_all.20 = f32[16,2,3584]{2,1,0:T(2,128)S(1)} all-to-all(f32[16,2,3584]{2,1,0:T(2,128)S(1)} %broadcast_in_dim.15), channel_id=1, replica_groups=mesh['row'=8,'col'=16] {'col'}, dimensions={0} | all-to-all | bytes 917504 | tf_op jit(solution)/shard_map/all_to_all | solution.py:11
  34.8 0.8 broadcast_in_dim.16
  35.7 5.3 all-to-all-start.1
  41.0 0.1 reduce_sum.58
  41.2 10.1 %all-to-all-done.1 = bf16[8,64,512]{2,1,0:T(8,128)(2,1)S(1)} async-done(((bf16[8,64,512]{2,1,0:T(8,128)(2,1)}), bf16[8,64,512]{2,1,0:T(8,128)(2,1)S(1)}, u32[]{:S(2)}, u32[]{:S(2)}) %all-to-all-start.1) | async-done | bytes 524320 | tf_op jit(solution)/shard_map/all_to_all | solution.py:11
  51.3 11.3 %fusion.12 = bf16[2,512,3584]{1,2,0:T(8,128)(2,1)} fusion(bf16[512,512,1]{1,0,2:T(8,128)(2,1)S(1)} %bitcast.52, f32[2,512,3584]{2,1,0:T(8,128)} %get-tuple-element.12, f32[2,3584]{1,0:T(2,128)S(1)} %fusion.30), kind=kOutput, calls=%fused_computation.23 | convolution fusion | flops 3769106432 | bytes 22573056 | tf_op jit(solution)/shard_map/td,pdf->ptf/dot_general | solution.py:55
  62.7 10.0 %copy.24 = bf16[2,512,3584]{2,1,0:T(8,128)(2,1)} copy(bf16[2,512,3584]{1,2,0:T(8,128)(2,1)} %fusion.12) | data formatting | bytes 14680064 | tf_op jit(solution)/shard_map/convert_element_type | solution.py:56
  72.7 0.2 all-gather.4.cloned.1.call-start
  72.9 0.5 all-gather.4.cloned.1.call-update
  73.4 619.7 %all-gather.6.cloned.1.call-done = bf16[32,512,3584]{2,1,0:T(8,128)(2,1)} async-done(((bf16[2,512,3584]{2,1,0:T(8,128)(2,1)}), bf16[32,512,3584]{2,1,0:T(8,128)(2,1)}) %all-gather.6.cloned.1.call-update) | async-done | bytes 117440528 | tf_op jit(solution)/shard_map/all_gather | solution.py:56
  693.1 41.3 %reduce_sum.59 = bf16[2,512,3584]{2,1,0:T(8,128)(2,1)} reduce(bf16[16,2,512,3584]{3,2,1,0:T(8,128)(2,1)} %bitcast.3, bf16[]{:T(256)} %constant.4.clone.1), dimensions={0}, to_apply=%region_2.0 | reduce | flops 55050240 | bytes 124780544 | tf_op jit(solution)/shard_map/reduce_sum | solution.py:56
  734.4 10.4 %convert_element_type.53 = f32[2,512,3584]{2,1,0:T(8,128)} convert(bf16[2,512,3584]{2,1,0:T(8,128)(2,1)} %reduce_sum.59) | non-fusion elementwise | flops 3670016 | bytes 22020096 | tf_op jit(solution)/shard_map/convert_element_type | solution.py:56
  744.8 9.8 %fusion.20 = (bf16[1,512,3584]{2,1,0:T(8,128)(2,1)S(1)}, bf16[1,512,3584]{2,1,0:T(8,128)(2,1)S(1)}, f32[512,3584]{1,0:T(8,128)}) fusion(bf16[512,3584]{1,0:T(8,128)(2,1)} %all-gather.4.cloned.1.call-done, f32[2,512,3584]{2,1,0:T(8,128)} %convert_element_type.53), kind=kLoop, calls=%fused_computation.28 | loop fusion | flops 25690112 | bytes 33030144 | tf_op jit(solution)/shard_map/stack | solution.py:64
  754.6 10.6 %fusion.1 = (f32[2,3584]{1,0:T(2,128)S(1)}, f32[2,3584,512]{1,2,0:T(8,128)}) fusion(f32[2,512,3584]{2,1,0:T(8,128)} %get-tuple-element.12, bf16[512,512,1]{1,0,2:T(8,128)(2,1)S(1)} %bitcast.53, bf16[1,512,3584]{2,1,0:T(8,128)(2,1)S(1)} %get-tuple-element.5, bf16[1,512,3584]{2,1,0:T(8,128)(2,1)S(1)} %get-tuple-element.4), kind=kOutput, calls=%fused_computation.3 | convolution fusion | flops 3769099264 | bytes 37253120 | tf_op jit(solution)/shard_map/td,ptf->pdf/dot_general | solution.py:65
  765.2 0.9 broadcast_in_dim.17
  766.0 5.2 all-to-all-start.2
  771.3 0.3 all-reduce.2.cloned.1.call-start
  771.6 10.3 %all-to-all-done.2 = f32[16,2,3584]{2,1,0:T(2,128)S(1)} async-done(((f32[16,2,3584]{2,1,0:T(2,128)}), f32[16,2,3584]{2,1,0:T(2,128)S(1)}, u32[]{:S(2)}, u32[]{:S(2)}) %all-to-all-start.2) | async-done | bytes 458784 | tf_op jit(solution)/shard_map/all_to_all | solution.py:11
  781.9 0.1 reduce_sum.61
  782.1 0.7 fusion.29
  782.7 14.1 %fusion.16 = bf16[2,64,3584]{2,1,0:T(8,128)(2,1)} fusion(bf16[2,64,512]{2,1,0:T(8,128)(2,1)S(1)} %copy-done.1, f32[2,3584,512]{1,2,0:T(8,128)} %get-tuple-element.14, f32[2,512,3584]{2,1,0:T(8,128)} %get-tuple-element.12, f32[2,3584]{1,0:T(2,128)S(1)} %get-tuple-element.10, f32[2,3584]{1,0:T(2,128)S(1)} %fusion.30), kind=kOutput, calls=%fused_computation.26 | convolution fusion | flops 2830041088 | bytes 30466048 | tf_op jit(solution)/shard_map/prd,pdf->prf/dot_general | solution.py:70
  796.8 14.2 %fusion.24 = bf16[2,64,512]{2,1,0:T(8,128)(2,1)S(1)} fusion(bf16[2,64,3584]{2,1,0:T(8,128)(2,1)S(1)} %copy-done, f32[2,3584,512]{1,2,0:T(8,128)} %get-tuple-element.14, f32[2,512,3584]{2,1,0:T(8,128)} %get-tuple-element.12, f32[2,3584]{1,0:T(2,128)S(1)} %get-tuple-element.10, f32[2,3584]{1,0:T(2,128)S(1)} %fusion.30), kind=kOutput, calls=%fused_computation.31 | convolution fusion | flops 2829647872 | bytes 30466048 | tf_op jit(solution)/shard_map/prf,pdf->prd/dot_general | solution.py:72
  811.0 1.1 broadcast_in_dim.18
  812.2 4.4 all-to-all-start.3
  816.6 11.5 %slice_bitcast_fusion.1 = (f32[512,3584]{1,0:T(8,128)}, f32[512,3584]{1,0:T(8,128)}) fusion(f32[2,512,3584]{2,1,0:T(8,128)} %convert_element_type.53), kind=kLoop, calls=%fused_computation.16 | loop fusion | bytes 29360128 | tf_op jit(solution)/shard_map/squeeze | solution.py:59
  828.0 2.1 fusion.27
  830.1 64.8 %all-reduce.2.cloned.1.call-done = bf16[2,64,3584]{2,1,0:T(8,128)(2,1)} async-done(((bf16[2,64,3584]{2,1,0:T(8,128)(2,1)}), bf16[2,64,3584]{2,1,0:T(8,128)(2,1)}) %all-reduce.2.cloned.1.call-update) | async-done | bytes 917520 | tf_op jit(solution)/shard_map/psum | solution.py:71
  894.9 2.6 convert_element_type.63
  897.5 0.8 convert_reduce_fusion
  (13 shorter events, 0.1 us)
Async XLA Ops:
  7.2 1.2 copy-start
  8.4 26.5 %copy-start.3 = (bf16[64,512]{1,0:T(8,128)(2,1)S(1)}, bf16[64,512]{1,0:T(8,128)(2,1)}, u32[]{:S(2)}) copy-start(bf16[64,512]{1,0:T(8,128)(2,1)} %param.6) | copy-start | bytes 196612
  8.4 32.8 %copy-start.2 = (f32[2,3584]{1,0:T(2,128)S(1)}, f32[2,3584]{1,0:T(2,128)}, u32[]{:S(2)}) copy-start(f32[2,3584]{1,0:T(2,128)} %param.10) | copy-start | bytes 86020
  35.7 15.6 %all-to-all-start.1 = ((bf16[8,64,512]{2,1,0:T(8,128)(2,1)}), bf16[8,64,512]{2,1,0:T(8,128)(2,1)S(1)}, u32[]{:S(2)}, u32[]{:S(2)}) async-start(bf16[8,64,512]{2,1,0:T(8,128)(2,1)} %broadcast_in_dim.16), calls=%async_computation.1 | async-start | bytes 1048576 | tf_op jit(solution)/shard_map/all_to_all | solution.py:11
  41.0 652.1 %all-gather.6.cloned.1.call-start = ((), (), s32[]{:S(2)}) async-start(), calls=%async_computation.6 | async-start | bytes 124780544 | tf_op jit(solution)/shard_map/all_gather | solution.py:56
  72.7 672.1 %all-gather.4.cloned.1.call-start = ((), (), s32[]{:S(2)}) async-start(), calls=%async_computation.4 | async-start | bytes 3899392 | tf_op jit(solution)/shard_map/all_gather | solution.py:62
  754.6 28.2 %copy-start.1 = (bf16[2,64,512]{2,1,0:T(8,128)(2,1)S(1)}, bf16[2,64,512]{2,1,0:T(8,128)(2,1)}, u32[]{:S(2)}) copy-start(bf16[2,64,512]{2,1,0:T(8,128)(2,1)} %param.8) | copy-start | bytes 393220
  766.0 15.9 %all-to-all-start.2 = ((f32[16,2,3584]{2,1,0:T(2,128)}), f32[16,2,3584]{2,1,0:T(2,128)S(1)}, u32[]{:S(2)}, u32[]{:S(2)}) async-start(f32[16,2,3584]{2,1,0:T(2,128)} %broadcast_in_dim.17), calls=%async_computation.2 | async-start | bytes 917504 | tf_op jit(solution)/shard_map/all_to_all | solution.py:11
  771.3 123.6 %all-reduce.2.cloned.1.call-start = ((), (), s32[]{:S(2)}) async-start(), calls=%async_computation.5 | async-start | bytes 1835008 | tf_op jit(solution)/shard_map/psum | solution.py:71
  812.2 85.4 %all-to-all-start.3 = ((bf16[8,2,64,512]{3,2,1,0:T(8,128)(2,1)}), bf16[8,2,64,512]{3,2,1,0:T(8,128)(2,1)S(1)}, u32[]{:S(2)}, u32[]{:S(2)}) async-start(bf16[8,2,64,512]{3,2,1,0:T(8,128)(2,1)} %broadcast_in_dim.18), calls=%async_computation.3 | async-start | bytes 2097152 | tf_op jit(solution)/shard_map/all_to_all | solution.py:11
Sparse Core Ops, SparseCore 0:
  72.8 620.2 all-gather.5
  695.2 49.0 all-gather.3
  811.2 83.7 all-reduce.1
